TPU v7x, 32 devices: a whole 2x2x4 slice. The times are simulated.
32 devices in a mesh: gx: 4 (over z), gy: 8 (over y, x, core).
Axes of the slice: x: 2, y: 2, z: 4, core: 2. Of those that a mesh axis runs over, the one named last changes fastest.
Arguments:
- orbitals: bfloat16 [24, 48, 11, 256], P('gx', 'gy'), may hold values from -140 to 140, as said below
- masses: float32 [24, 48, 11], P('gx', 'gy'), may hold values from 0.5 to 2, as said below
- cell_matrices: bfloat16 [4, 8, 2, 216, 216], P('gx', 'gy'), may hold values from -0.12 to 3.12, as said below
Outputs:
- filtered_orbitals: bfloat16 [24, 48, 11, 256], P('gx', 'gy')
Inputs may be any that keep to these rules, and one draw needn't show every extreme that they name: Entries of orbitals that hold the same mesh node are equal. Entries of masses that hold the same mesh node are equal. `cell_matrices`: every cell matrix is symmetric.
All inputs are finite; a program needn't handle non-finite values.
Results may differ from a plain program's by a relative error of at most 0.0063.
The roundings to bfloat16 on the way count: a program that leaves them out, or rounds other values in their place, can miss the bound.
Values sent between devices are 32-bit elements; how exact they have to be, the bound alone decides.
A program may use at most 64 MiB of HBM per device.

v0:
```python
import jax
import jax.numpy as jnp
from jax import lax
from jax.sharding import PartitionSpec as P

FILTER_DEG = 3
NS_STEPS = 2


center_shift = 12.0
half_span = 12.0


def with_halo(array, sides, width):
    for axis, dim in sides:
        size, length = (lax.axis_size(axis), array.shape[dim])
        up = [(i, (i + 1) % size) for i in range(size)]
        down = [(j, i) for i, j in up]
        last = lax.slice_in_dim(array, length - width, length, axis=dim)
        leading = lax.slice_in_dim(array, 0, width, axis=dim)
        before = lax.ppermute(last, axis, up)
        after = lax.ppermute(leading, axis, down)
        array = jnp.concatenate([before, array, after], axis=dim)
    return array


def unfold_cells(values, along_dim, cells_along):
    moved = jnp.moveaxis(values, along_dim, 0)
    trailing = moved.shape[1:]
    main_part = moved[: 5 * cells_along].reshape((cells_along, 5) + trailing)
    far_layer = moved[5::5][:, None]
    window = jnp.concatenate([main_part, far_layer], 1)
    return jnp.moveaxis(window, (0, 1), (along_dim, along_dim + 1))


def fold_cells(window, along_dim, cells_along):
    moved = jnp.moveaxis(window, (along_dim, along_dim + 1), (0, 1))
    trailing = moved.shape[2:]
    leading = jnp.concatenate([moved[:, :5], jnp.zeros((1, 5) + trailing, moved.dtype)], 0)
    carried = jnp.concatenate([jnp.zeros((1,) + trailing, moved.dtype), moved[:, 5]], 0)
    leading = leading.at[:, 0].add(carried)
    flattened = leading.reshape((5 * (cells_along + 1),) + trailing)[: 5 * cells_along + 1]
    return jnp.moveaxis(flattened, 0, along_dim)


def to_cells(values, cells_x, cells_y, cells_z):
    window = unfold_cells(values, 0, cells_x)
    window = unfold_cells(window, 2, cells_y)
    window = unfold_cells(window, 4, cells_z)
    window = jnp.transpose(window, (0, 2, 4, 1, 3, 5, 6))
    return window.reshape((cells_x, cells_y, cells_z, 216, window.shape[-1]))


def from_cells(products, cells_x, cells_y, cells_z):
    window = products.reshape((cells_x, cells_y, cells_z, 6, 6, 6, products.shape[-1]))
    window = jnp.transpose(window, (0, 3, 1, 4, 2, 5, 6))
    window = fold_cells(window, 4, cells_z)
    window = fold_cells(window, 2, cells_y)
    return fold_cells(window, 0, cells_x)


def inverse_root(intersection):
    frob_norm = jnp.sqrt(jnp.sum(intersection * intersection))
    current = intersection / frob_norm
    identity = jnp.eye(intersection.shape[0], dtype=jnp.float32)
    factor_z = identity
    for sweep_index in range(NS_STEPS):
        step_t = 1.5 * identity - 0.5 * jnp.dot(factor_z, current, precision=lax.Precision.HIGHEST)
        current = jnp.dot(current, step_t, precision=lax.Precision.HIGHEST)
        factor_z = jnp.dot(step_t, factor_z, precision=lax.Precision.HIGHEST)
    return factor_z / jnp.sqrt(frob_norm)


def body(orbitals, masses, cell_matrices):
    cells_x, cells_y, cells_z = cell_matrices.shape[:3]
    orb_count = orbitals.shape[3]

    def apply_operator(rounded):
        cell_vectors = to_cells(rounded, cells_x, cells_y, cells_z)
        products = jnp.einsum(
            "abcij,abcjo->abcio", cell_matrices, cell_vectors, preferred_element_type=jnp.float32
        )
        partial_value = from_cells(products, cells_x, cells_y, cells_z)
        padded = with_halo(partial_value, (("gx", 0), ("gy", 1)), 1)
        summed = partial_value.at[0].add(padded[0, 1:-1]).at[-1].add(padded[-1, 1:-1])
        summed = summed.at[:, 0].add(padded[1:-1, 0]).at[:, -1].add(padded[1:-1, -1])
        summed = summed.at[0, 0].add(padded[0, 0]).at[0, -1].add(padded[0, -1])
        summed = summed.at[-1, 0].add(padded[-1, 0]).at[-1, -1].add(padded[-1, -1])
        return summed / masses[..., None]

    starting = orbitals.astype(jnp.float32)
    previous = starting
    current = (apply_operator(orbitals) - center_shift * starting) / half_span
    for sweep_index in range(FILTER_DEG - 1):
        following = (
            2.0
            * (apply_operator(current.astype(jnp.bfloat16)) - center_shift * current)
            / half_span
            - previous
        )
        previous = current
        current = following
    owned_rows = current[:-1, :-1].reshape((-1, orb_count))
    owned_mass = masses[:-1, :-1].reshape((-1, 1))
    local_intersection = jnp.einsum(
        "no,np->op", owned_rows * owned_mass, owned_rows, precision=lax.Precision.HIGHEST
    )
    node_total = (
        (current.shape[0] - 1)
        * lax.axis_size("gx")
        * (current.shape[1] - 1)
        * lax.axis_size("gy")
        * current.shape[2]
    )
    row_sum = lax.psum(local_intersection, "gy")
    intersection_sum = lax.psum(row_sum, "gx")
    intersection = intersection_sum / node_total
    factor = inverse_root(intersection)
    node_rows = current.reshape((-1, orb_count))
    result = jnp.dot(node_rows, factor, precision=lax.Precision.HIGHEST).astype(jnp.bfloat16)
    return result.reshape(current.shape)


def solution(mesh):
    return jax.shard_map(
        body,
        mesh=mesh,
        in_specs=(P("gx", "gy", None, None), P("gx", "gy", None), P("gx", "gy", None, None, None)),
        out_specs=P("gx", "gy", None, None),
        check_vma=False,
    )
```

profile of v0, /device:TPU:0, one launch (start us, length us, event | category | flops | bytes accessed | tf_op | source)
XLA Modules:
  0.0 195.6 jit_solution(4431525838171367299)
XLA Ops:
  6.5 1.0 copy-done.1
  8.3 0.3 pad_maximum_fusion
  9.6 0.6 copy.62
  10.7 0.5 copy-done.2
  11.4 0.6 slice-done.1
  12.4 0.7 copy.65
  14.5 3.1 %collective-permute-start = (f32[1,6,11,256]{3,2,1,0:T(8,128)S(1)}, f32[1,6,11,256]{3,2,1,0:T(8,128)S(1)}, u32[]{:S(2)}, u32[]{:S(2)}) collective-permute-start(f32[1,6,11,256]{3,2,1,0:T(8,128)S(1)} %slice.1363), channel_id=1, source_target_pairs={{0,8},{8,16},{16,24},{24,0},{1,9},{9,17},{17,25},{25,1},{2,10},{10... | collective-permute-start | bytes 202760 | tf_op jit(solution)/shard_map/ppermute | solution.py:21
  17.7 0.6 copy-done.7
  18.3 0.7 and_reduce_fusion
  19.0 3.4 %collective-permute-done = f32[1,6,11,256]{3,2,1,0:T(8,128)S(1)} collective-permute-done((f32[1,6,11,256]{3,2,1,0:T(8,128)S(1)}, f32[1,6,11,256]{3,2,1,0:T(8,128)S(1)}, u32[]{:S(2)}, u32[]{:S(2)}) %collective-permute-start) | collective-permute-done | bytes 67616 | tf_op jit(solution)/shard_map/ppermute | solution.py:21
  22.4 1.9 collective-permute-start.1
  24.3 0.6 fusion.50
  24.8 2.2 %collective-permute-done.1 = f32[1,6,11,256]{3,2,1,0:T(8,128)S(1)} collective-permute-done((f32[1,6,11,256]{3,2,1,0:T(8,128)S(1)}, f32[1,6,11,256]{3,2,1,0:T(8,128)S(1)}, u32[]{:S(2)}, u32[]{:S(2)}) %collective-permute-start.1) | collective-permute-done | bytes 67616 | tf_op jit(solution)/shard_map/ppermute | solution.py:22
  27.1 2.6 %collective-permute-start.3 = (f32[8,1,11,256]{3,2,1,0:T(8,128)S(1)}, f32[8,1,11,256]{3,2,1,0:T(8,128)S(1)}, u32[]{:S(2)}, u32[]{:S(2)}) collective-permute-start(f32[8,1,11,256]{3,2,1,0:T(8,128)S(1)} %get-tuple-element.411), channel_id=1, source_target_pairs={{1,0},{2,1},{3,2},{4,3},{5,4},{6,5},{7,6},{0,7},{9,8},{10,9},{11,1... | collective-permute-start | bytes 270344 | tf_op jit(solution)/shard_map/ppermute | solution.py:22
  29.8 2.6 %collective-permute-done.2 = f32[8,1,11,256]{3,2,1,0:T(8,128)S(1)} collective-permute-done((f32[8,1,11,256]{3,2,1,0:T(8,128)S(1)}, f32[8,1,11,256]{3,2,1,0:T(8,128)S(1)}, u32[]{:S(2)}, u32[]{:S(2)}) %collective-permute-start.2) | collective-permute-done | bytes 90144 | tf_op jit(solution)/shard_map/ppermute | solution.py:21
  32.5 1.9 fusion.32
  34.5 0.7 copy-done.5
  37.2 0.6 copy.76
  38.3 0.5 copy-done.3
  39.1 0.6 slice-done.2
  40.0 0.7 copy.79
  42.3 7.1 %collective-permute-done.4 = f32[1,6,11,256]{3,2,1,0:T(8,128)S(1)} collective-permute-done((f32[1,6,11,256]{3,2,1,0:T(8,128)S(1)}, f32[1,6,11,256]{3,2,1,0:T(8,128)S(1)}, u32[]{:S(2)}, u32[]{:S(2)}) %collective-permute-start.4) | collective-permute-done | bytes 67616 | tf_op jit(solution)/shard_map/ppermute | solution.py:21
  49.4 1.9 collective-permute-start.5
  51.3 3.0 %collective-permute-done.5 = f32[1,6,11,256]{3,2,1,0:T(8,128)S(1)} collective-permute-done((f32[1,6,11,256]{3,2,1,0:T(8,128)S(1)}, f32[1,6,11,256]{3,2,1,0:T(8,128)S(1)}, u32[]{:S(2)}, u32[]{:S(2)}) %collective-permute-start.5) | collective-permute-done | bytes 67616 | tf_op jit(solution)/shard_map/ppermute | solution.py:22
  54.4 2.6 %collective-permute-start.7 = (f32[8,1,11,256]{3,2,1,0:T(8,128)S(1)}, f32[8,1,11,256]{3,2,1,0:T(8,128)S(1)}, u32[]{:S(2)}, u32[]{:S(2)}) collective-permute-start(f32[8,1,11,256]{3,2,1,0:T(8,128)S(1)} %get-tuple-element.409), channel_id=1, source_target_pairs={{1,0},{2,1},{3,2},{4,3},{5,4},{6,5},{7,6},{0,7},{9,8},{10,9},{11,1... | collective-permute-start | bytes 270344 | tf_op jit(solution)/shard_map/ppermute | solution.py:22
  57.0 3.1 %collective-permute-done.6 = f32[8,1,11,256]{3,2,1,0:T(8,128)S(1)} collective-permute-done((f32[8,1,11,256]{3,2,1,0:T(8,128)S(1)}, f32[8,1,11,256]{3,2,1,0:T(8,128)S(1)}, u32[]{:S(2)}, u32[]{:S(2)}) %collective-permute-start.6) | collective-permute-done | bytes 90144 | tf_op jit(solution)/shard_map/ppermute | solution.py:21
  60.2 1.9 fusion.33
  64.3 0.6 copy.89
  65.4 0.5 copy-done.4
  66.2 0.6 slice-done.3
  67.1 0.7 copy.92
  69.4 7.0 %collective-permute-done.8 = f32[1,6,11,256]{3,2,1,0:T(8,128)S(1)} collective-permute-done((f32[1,6,11,256]{3,2,1,0:T(8,128)S(1)}, f32[1,6,11,256]{3,2,1,0:T(8,128)S(1)}, u32[]{:S(2)}, u32[]{:S(2)}) %collective-permute-start.8) | collective-permute-done | bytes 67616 | tf_op jit(solution)/shard_map/ppermute | solution.py:21
  76.3 2.0 %collective-permute-start.9 = (f32[1,6,11,256]{3,2,1,0:T(8,128)S(1)}, f32[1,6,11,256]{3,2,1,0:T(8,128)S(1)}, u32[]{:S(2)}, u32[]{:S(2)}) collective-permute-start(f32[1,6,11,256]{3,2,1,0:T(8,128)S(1)} %get-tuple-element.401), channel_id=1, source_target_pairs={{8,0},{16,8},{24,16},{0,24},{9,1},{17,9},{25,17},{1,25},{10,2},{18... | collective-permute-start | bytes 202760 | tf_op jit(solution)/shard_map/ppermute | solution.py:22
  78.4 2.9 %collective-permute-done.9 = f32[1,6,11,256]{3,2,1,0:T(8,128)S(1)} collective-permute-done((f32[1,6,11,256]{3,2,1,0:T(8,128)S(1)}, f32[1,6,11,256]{3,2,1,0:T(8,128)S(1)}, u32[]{:S(2)}, u32[]{:S(2)}) %collective-permute-start.9) | collective-permute-done | bytes 67616 | tf_op jit(solution)/shard_map/ppermute | solution.py:22
  81.3 2.6 %collective-permute-start.11 = (f32[8,1,11,256]{3,2,1,0:T(8,128)S(1)}, f32[8,1,11,256]{3,2,1,0:T(8,128)S(1)}, u32[]{:S(2)}, u32[]{:S(2)}) collective-permute-start(f32[8,1,11,256]{3,2,1,0:T(8,128)S(1)} %get-tuple-element.407), channel_id=1, source_target_pairs={{1,0},{2,1},{3,2},{4,3},{5,4},{6,5},{7,6},{0,7},{9,8},{10,9},{11,1... | collective-permute-start | bytes 270344 | tf_op jit(solution)/shard_map/ppermute | solution.py:22
  84.0 3.9 %collective-permute-done.10 = f32[8,1,11,256]{3,2,1,0:T(8,128)S(1)} collective-permute-done((f32[8,1,11,256]{3,2,1,0:T(8,128)S(1)}, f32[8,1,11,256]{3,2,1,0:T(8,128)S(1)}, u32[]{:S(2)}, u32[]{:S(2)}) %collective-permute-start.10) | collective-permute-done | bytes 90144 | tf_op jit(solution)/shard_map/ppermute | solution.py:21
  87.9 1.9 fusion.34
  89.9 0.4 multiply_subtract_fusion
  90.3 1.9 convolution_bitcast_fusion.3
  92.2 53.8 %all-reduce.21.cloned.1.call-done = f32[256,256]{1,0:T(8,128)} async-done(((f32[256,256]{1,0:T(8,128)}), f32[256,256]{1,0:T(8,128)}) %all-reduce.21.cloned.1.call-update) | async-done | bytes 262160 | tf_op jit(solution)/shard_map/psum | solution.py:115
  146.1 37.1 %all-reduce.23.cloned.1.call-done = f32[256,256]{1,0:T(8,128)} async-done(((f32[256,256]{1,0:T(8,128)}), f32[256,256]{1,0:T(8,128)}) %all-reduce.23.cloned.1.call-update) | async-done | bytes 262160 | tf_op jit(solution)/shard_map/psum | solution.py:116
  183.2 1.7 multiply_reduce_fusion
  185.6 0.3 fusion.1
  186.2 0.4 fusion.31
  186.6 0.4 fusion
  187.0 0.4 convolution_divide_fusion
  187.4 0.5 convolution_convert_fusion
  188.0 0.8 copy.95
  (160 shorter events, 14.0 us)
Async XLA Ops:
  6.5 2.0 %copy-start = (bf16[1,1,2,216,216]{4,3,2,1,0:T(8,128)(2,1)S(1)}, bf16[1,1,2,216,216]{4,3,2,1,0:T(8,128)(2,1)}, u32[]{:S(2)}) copy-start(bf16[1,1,2,216,216]{4,3,2,1,0:T(8,128)(2,1)} %param.71) | copy-start | bytes 559876
  6.5 1.0 copy-start.1
  6.5 1.1 slice-start
  6.5 139.5 %all-reduce.21.cloned.1.call-start = ((), (), s32[]{:S(2)}) async-start(), calls=%async_computation | async-start | bytes 524288 | tf_op jit(solution)/shard_map/psum | solution.py:115
  10.4 0.8 copy-start.2
  11.2 0.9 slice-start.1
  14.5 7.9 %collective-permute-start = (f32[1,6,11,256]{3,2,1,0:T(8,128)S(1)}, f32[1,6,11,256]{3,2,1,0:T(8,128)S(1)}, u32[]{:S(2)}, u32[]{:S(2)}) collective-permute-start(f32[1,6,11,256]{3,2,1,0:T(8,128)S(1)} %slice.1363), channel_id=1, source_target_pairs={{0,8},{8,16},{16,24},{24,0},{1,9},{9,17},{17,25},{25,1},{2,10},{10... | collective-permute-start | bytes 202760 | tf_op jit(solution)/shard_map/ppermute | solution.py:21
  17.6 0.7 copy-start.7
  22.4 4.7 %collective-permute-start.1 = (f32[1,6,11,256]{3,2,1,0:T(8,128)S(1)}, f32[1,6,11,256]{3,2,1,0:T(8,128)S(1)}, u32[]{:S(2)}, u32[]{:S(2)}) collective-permute-start(f32[1,6,11,256]{3,2,1,0:T(8,128)S(1)} %get-tuple-element.405), channel_id=1, source_target_pairs={{8,0},{16,8},{24,16},{0,24},{9,1},{17,9},{25,17},{1,25},{10,2},{18... | collective-permute-start | bytes 202760 | tf_op jit(solution)/shard_map/ppermute | solution.py:22
  27.1 5.3 %collective-permute-start.2 = (f32[8,1,11,256]{3,2,1,0:T(8,128)S(1)}, f32[8,1,11,256]{3,2,1,0:T(8,128)S(1)}, u32[]{:S(2)}, u32[]{:S(2)}) collective-permute-start(f32[8,1,11,256]{3,2,1,0:T(8,128)S(1)} %get-tuple-element.412), channel_id=1, source_target_pairs={{0,1},{1,2},{2,3},{3,4},{4,5},{5,6},{6,7},{7,0},{8,9},{9,10},{10,1... | collective-permute-start | bytes 270344 | tf_op jit(solution)/shard_map/ppermute | solution.py:21
  27.1 5.3 %collective-permute-start.3 = (f32[8,1,11,256]{3,2,1,0:T(8,128)S(1)}, f32[8,1,11,256]{3,2,1,0:T(8,128)S(1)}, u32[]{:S(2)}, u32[]{:S(2)}) collective-permute-start(f32[8,1,11,256]{3,2,1,0:T(8,128)S(1)} %get-tuple-element.411), channel_id=1, source_target_pairs={{1,0},{2,1},{3,2},{4,3},{5,4},{6,5},{7,6},{0,7},{9,8},{10,9},{11,1... | collective-permute-start | bytes 270344 | tf_op jit(solution)/shard_map/ppermute | solution.py:22
  34.5 0.7 copy-start.5
  38.1 0.8 copy-start.3
  38.9 0.9 slice-start.2
  42.1 7.3 %collective-permute-start.4 = (f32[1,6,11,256]{3,2,1,0:T(8,128)S(1)}, f32[1,6,11,256]{3,2,1,0:T(8,128)S(1)}, u32[]{:S(2)}, u32[]{:S(2)}) collective-permute-start(f32[1,6,11,256]{3,2,1,0:T(8,128)S(1)} %slice.1391), channel_id=1, source_target_pairs={{0,8},{8,16},{16,24},{24,0},{1,9},{9,17},{17,25},{25,1},{2,10},{10... | collective-permute-start | bytes 202760 | tf_op jit(solution)/shard_map/ppermute | solution.py:21
  49.4 4.9 %collective-permute-start.5 = (f32[1,6,11,256]{3,2,1,0:T(8,128)S(1)}, f32[1,6,11,256]{3,2,1,0:T(8,128)S(1)}, u32[]{:S(2)}, u32[]{:S(2)}) collective-permute-start(f32[1,6,11,256]{3,2,1,0:T(8,128)S(1)} %get-tuple-element.403), channel_id=1, source_target_pairs={{8,0},{16,8},{24,16},{0,24},{9,1},{17,9},{25,17},{1,25},{10,2},{18... | collective-permute-start | bytes 202760 | tf_op jit(solution)/shard_map/ppermute | solution.py:22
  54.3 5.8 %collective-permute-start.6 = (f32[8,1,11,256]{3,2,1,0:T(8,128)S(1)}, f32[8,1,11,256]{3,2,1,0:T(8,128)S(1)}, u32[]{:S(2)}, u32[]{:S(2)}) collective-permute-start(f32[8,1,11,256]{3,2,1,0:T(8,128)S(1)} %get-tuple-element.410), channel_id=1, source_target_pairs={{0,1},{1,2},{2,3},{3,4},{4,5},{5,6},{6,7},{7,0},{8,9},{9,10},{10,1... | collective-permute-start | bytes 270344 | tf_op jit(solution)/shard_map/ppermute | solution.py:21
  54.4 5.8 %collective-permute-start.7 = (f32[8,1,11,256]{3,2,1,0:T(8,128)S(1)}, f32[8,1,11,256]{3,2,1,0:T(8,128)S(1)}, u32[]{:S(2)}, u32[]{:S(2)}) collective-permute-start(f32[8,1,11,256]{3,2,1,0:T(8,128)S(1)} %get-tuple-element.409), channel_id=1, source_target_pairs={{1,0},{2,1},{3,2},{4,3},{5,4},{6,5},{7,6},{0,7},{9,8},{10,9},{11,1... | collective-permute-start | bytes 270344 | tf_op jit(solution)/shard_map/ppermute | solution.py:22
  65.2 0.8 copy-start.4
  65.9 0.9 slice-start.3
  69.2 7.1 %collective-permute-start.8 = (f32[1,6,11,256]{3,2,1,0:T(8,128)S(1)}, f32[1,6,11,256]{3,2,1,0:T(8,128)S(1)}, u32[]{:S(2)}, u32[]{:S(2)}) collective-permute-start(f32[1,6,11,256]{3,2,1,0:T(8,128)S(1)} %slice.1419), channel_id=1, source_target_pairs={{0,8},{8,16},{16,24},{24,0},{1,9},{9,17},{17,25},{25,1},{2,10},{10... | collective-permute-start | bytes 202760 | tf_op jit(solution)/shard_map/ppermute | solution.py:21
  76.3 4.9 %collective-permute-start.9 = (f32[1,6,11,256]{3,2,1,0:T(8,128)S(1)}, f32[1,6,11,256]{3,2,1,0:T(8,128)S(1)}, u32[]{:S(2)}, u32[]{:S(2)}) collective-permute-start(f32[1,6,11,256]{3,2,1,0:T(8,128)S(1)} %get-tuple-element.401), channel_id=1, source_target_pairs={{8,0},{16,8},{24,16},{0,24},{9,1},{17,9},{25,17},{1,25},{10,2},{18... | collective-permute-start | bytes 202760 | tf_op jit(solution)/shard_map/ppermute | solution.py:22
  81.3 6.6 %collective-permute-start.10 = (f32[8,1,11,256]{3,2,1,0:T(8,128)S(1)}, f32[8,1,11,256]{3,2,1,0:T(8,128)S(1)}, u32[]{:S(2)}, u32[]{:S(2)}) collective-permute-start(f32[8,1,11,256]{3,2,1,0:T(8,128)S(1)} %get-tuple-element.408), channel_id=1, source_target_pairs={{0,1},{1,2},{2,3},{3,4},{4,5},{5,6},{6,7},{7,0},{8,9},{9,10},{10,1... | collective-permute-start | bytes 270344 | tf_op jit(solution)/shard_map/ppermute | solution.py:21
  81.3 6.6 %collective-permute-start.11 = (f32[8,1,11,256]{3,2,1,0:T(8,128)S(1)}, f32[8,1,11,256]{3,2,1,0:T(8,128)S(1)}, u32[]{:S(2)}, u32[]{:S(2)}) collective-permute-start(f32[8,1,11,256]{3,2,1,0:T(8,128)S(1)} %get-tuple-element.407), channel_id=1, source_target_pairs={{1,0},{2,1},{3,2},{4,3},{5,4},{6,5},{7,6},{0,7},{9,8},{10,9},{11,1... | collective-permute-start | bytes 270344 | tf_op jit(solution)/shard_map/ppermute | solution.py:22
  92.2 91.0 %all-reduce.23.cloned.1.call-start = ((), (), s32[]{:S(2)}) async-start(), calls=%async_computation.1 | async-start | bytes 524288 | tf_op jit(solution)/shard_map/psum | solution.py:116
  183.2 2.4 %copy-start.6 = (f32[256,256]{1,0:T(8,128)S(1)}, f32[256,256]{1,0:T(8,128)}, u32[]{:S(2)}) copy-start(f32[256,256]{1,0:T(8,128)} %all-reduce.23.cloned.1.call-done) | copy-start | bytes 786436
Sparse Core Ops, SparseCore 0:
  92.3 53.6 all-reduce.20
  148.4 34.6 all-reduce.22
where the time goes:
time: 196 us
  waiting for transfers between devices  126 us (64%)
  local copies, waits for them, and re-layouts  21 us (11%)
  starting transfers between devices  17.1 us (9%)
  between operations  15.3 us (8%)
  other arithmetic  11.6 us (6%)
  matrix products  4.74 us (2%)
    psum x1, waiting for transfers between devices, body(): row_sum = lax.psum(local_intersection, 'gy')  53.8 us
    psum x1, waiting for transfers between devices, body(): intersection_sum = lax.psum(row_sum, 'gx')  37.1 us
    ppermute x6, waiting for transfers between devices, with_halo(): before = lax.ppermute(last, axis, up)  27 us
    ppermute x6, starting transfers between devices, with_halo(): after = lax.ppermute(leading, axis, down)  13.6 us
    ppermute x6, waiting for transfers between devices, with_halo(): after = lax.ppermute(leading, axis, down)  8.1 us
    scatter-add x6, other arithmetic, apply_operator(): summed = summed.at[0, 0].add(padded[0, 0]).at[0, -1].add(padded[0, -1])  5.81 us
    unnamed x26, local copies, waits for them, and re-layouts  5.14 us
    scatter-add x9, local copies, waits for them, and re-layouts, fold_cells(): leading = leading.at[:, 0].add(carried)  4.14 us
  transfers between devices with their start and end apart: 14, of which 11 were waited for; matrix products, arithmetic and copies ran while one was open for 1% of the time, Pallas kernels for 0%

commit v1 on v0

v1 whole, which is shorter than its diff:
```python
import functools

import jax
import jax.numpy as jnp
import numpy as np
from jax import lax
from jax.experimental import pallas as pl
from jax.experimental.pallas import tpu as pltpu
from jax.sharding import PartitionSpec as P

FILTER_DEG = 3
CENTER_SHIFT = 12.0
HALF_SPAN = 12.0

RIM = 256
ROWS = 448
INNER = ROWS - RIM
SIDE = 80
CORNER = 16
BF16 = jnp.bfloat16
F32 = jnp.float32

MESSAGES = (
    (-1, 0, 0, SIDE),
    (1, 0, 128, SIDE),
    (0, 1, 64, SIDE),
    (0, -1, 192, SIDE),
    (-1, -1, 0, CORNER),
    (-1, 1, 64, CORNER),
    (1, 1, 128, CORNER),
    (1, -1, 192, CORNER),
)


def column_starts():
    starts = {(0, 0): 0, (0, 5): 64, (5, 5): 128, (5, 0): 192}
    for i in range(4):
        starts[(0, i + 1)] = 16 + 12 * i
        starts[(i + 1, 5)] = 80 + 12 * i
        starts[(5, i + 1)] = 144 + 12 * i
        starts[(i + 1, 0)] = 208 + 12 * i
    for i in range(4):
        for j in range(4):
            starts[(i + 1, j + 1)] = RIM + 12 * (4 * i + j)
    return starts


STARTS = column_starts()


def tables():
    to_rows = np.zeros((2, ROWS, 216), np.float32)
    to_columns = np.zeros((2, 216, ROWS), np.float32)
    pick_xy = np.zeros((ROWS, 48), np.float32)
    pick_z = np.zeros((3, ROWS, 128), np.float32)
    pick_z[2] = 1.0
    for (x, y), start in STARTS.items():
        for half in range(2):
            for k in range(6):
                row = start + 6 * half + k
                z = 5 * half + k
                for cell in range(2):
                    if 0 <= z - 5 * cell <= 5:
                        to_rows[cell, row, (x * 6 + y) * 6 + z - 5 * cell] = 1
                to_columns[half, (x * 6 + y) * 6 + k, row] = 1
                pick_xy[row, 8 * x + y] = 1
                pick_z[0, row, z] = 1
                pick_z[2, row, :] = 0
                if x < 5 and y < 5 and not (half == 1 and k == 0):
                    pick_z[1, row, z] = 1
    return (
        to_rows.astype(BF16),
        to_columns.astype(BF16),
        pick_xy,
        pick_z,
    )


def dot(a, b):
    return jnp.dot(a, b, preferred_element_type=F32)


def dot_rows(a, b):
    return lax.dot_general(a, b, (((0,), (0,)), ((), ())), preferred_element_type=F32)


def split(a):
    high = a.astype(BF16)
    return high, (a - high.astype(F32)).astype(BF16)


def dot3(a, b):
    a_high, a_low = split(a)
    b_high, b_low = split(b)
    return dot(a_high, b_high) + (dot(a_high, b_low) + dot(a_low, b_high))


def gram(rows, weight):
    a_high, a_low = split(rows * weight)
    b_high, b_low = split(rows)

    def part(lanes, columns):
        return dot_rows(a_high[:, lanes], b_high[:, columns]) + (
            dot_rows(a_high[:, lanes], b_low[:, columns])
            + dot_rows(a_low[:, lanes], b_high[:, columns])
        )

    top = part(slice(0, 128), slice(0, 256))
    return top[:, :128], top[:, 128:], part(slice(128, 256), slice(128, 256))


def inverse_root(stacked, node_total):
    s00, s01, s11 = stacked[0:128], stacked[128:256], stacked[256:384]
    top = jnp.concatenate([s00, s01], axis=1)
    bottom = jnp.concatenate([s01.T, s11], axis=1)
    inter = jnp.concatenate([top, bottom], axis=0) * (1.0 / node_total)
    frob2 = jnp.sum(jnp.sum(inter * inter, axis=1, keepdims=True), axis=0, keepdims=True)
    frob = jnp.sqrt(frob2)
    current = inter / frob
    row_id = lax.broadcasted_iota(jnp.int32, (256, 256), 0)
    col_id = lax.broadcasted_iota(jnp.int32, (256, 256), 1)
    identity = jnp.where(row_id == col_id, 1.0, 0.0).astype(F32)
    square = dot3(current, current)
    tail = 1.6875 * identity - 0.5625 * current + 0.0625 * square
    factor_z = 2.25 * identity - 2.4375 * current + dot3(square, tail)
    return factor_z / jnp.sqrt(frob)


def filter_phase(sizes, orbitals, masses, cells, to_rows, to_columns, pick_xy, pick_z,
                 matrix, mass_pad, states, rounded, sent, arrived, send_sems, recv_sems,
                 before_first_send):
    n_gx, n_gy = sizes
    my_x, my_y = lax.axis_index("gx"), lax.axis_index("gy")

    states[0] = jnp.zeros((ROWS, 256), F32)
    for (x, y), start in STARTS.items():
        column = orbitals[x, y].astype(F32)
        states[0, start : start + 6] = column[0:6]
        states[0, start + 6 : start + 12] = column[5:11]
    rounded[...] = states[0].astype(BF16)

    first = dot(to_rows[0], cells[0, 0, 0]).astype(BF16)
    second = dot(to_rows[1], cells[0, 0, 1]).astype(BF16)
    matrix[...] = (dot(first, to_columns[0]) + dot(second, to_columns[1])).astype(BF16)

    mass_pad[...] = jnp.zeros(mass_pad.shape, F32)
    for x in range(6):
        mass_pad[8 * x : 8 * x + 6, 0:11] = masses[x]
    spread = jnp.dot(
        pick_xy[...], mass_pad[...], preferred_element_type=F32, precision=lax.Precision.HIGHEST
    )
    mass = jnp.sum(spread * pick_z[0], axis=1, keepdims=True) + pick_z[2, :, 0:1]
    weight = jnp.sum(spread * pick_z[1], axis=1, keepdims=True)
    scale1 = 1.0 / (HALF_SPAN * mass)
    shift = CENTER_SHIFT / HALF_SPAN

    def copies(step):
        out = []
        for index, (dx, dy, first_row, rows) in enumerate(MESSAGES):
            target = (lax.rem(my_x + dx + n_gx, n_gx), lax.rem(my_y + dy + n_gy, n_gy))
            landing = arrived.at[step, pl.ds(80 * index, rows)] if rows == SIDE else arrived.at[
                step, pl.ds(320 + 16 * (index - 4), rows)
            ]
            out.append(
                pltpu.make_async_remote_copy(
                    src_ref=sent.at[step, pl.ds(first_row, rows)],
                    dst_ref=landing,
                    send_sem=send_sems.at[step, index],
                    recv_sem=recv_sems.at[step, index],
                    device_id=target,
                    device_id_type=pl.DeviceIdType.MESH,
                )
            )
        return out

    def received(step, index, low, high):
        base = 80 * index if index < 4 else 320 + 16 * (index - 4)
        return arrived[step, base + low : base + high]

    def advance(step, product, rows):
        if step == 0:
            return product * scale1[rows] - shift * states[0, rows]
        return (2.0 * product) * scale1[rows] - (2.0 * shift) * states[step, rows] - states[step - 1, rows]

    rim, inner = slice(0, RIM), slice(RIM, ROWS)
    ahead = dot(matrix[rim, inner], rounded[inner])
    grams = None
    everything = []
    for step in range(FILTER_DEG):
        product = ahead + dot(matrix[rim, rim], rounded[rim])
        sent[step, 0:RIM] = product
        sent[step, RIM : RIM + CORNER] = product[0:CORNER]
        if step == 0:
            before_first_send()
        moves = copies(step)
        everything += moves
        for move in moves:
            move.start()
        last = step == FILTER_DEG - 1
        inner_next = advance(step, dot(matrix[inner], rounded[...]), inner)
        states[step + 1, inner] = inner_next
        if last:
            grams = gram(inner_next, weight[inner])
        else:
            rounded[inner] = inner_next.astype(BF16)
            ahead = dot(matrix[rim, inner], rounded[inner])
        for move in moves:
            move.wait_recv()
        own = lambda low, high: sent[step, low:high]
        got = functools.partial(received, step)
        summed = jnp.concatenate(
            [
                own(0, 16) + got(1, 64, 80) + got(2, 0, 16) + got(6, 0, 16),
                own(16, 64) + got(1, 16, 64),
                own(64, 80) + got(1, 0, 16) + got(3, 64, 80) + got(7, 0, 16),
                own(80, 128) + got(3, 16, 64),
                own(128, 144) + got(0, 64, 80) + got(3, 0, 16) + got(4, 0, 16),
                own(144, 192) + got(0, 16, 64),
                own(192, 208) + got(0, 0, 16) + got(2, 64, 80) + got(5, 0, 16),
                own(208, 256) + got(2, 16, 64),
            ],
            axis=0,
        )
        rim_next = advance(step, summed, rim)
        states[step + 1, rim] = rim_next
        if last:
            owned = jnp.concatenate([rim_next[0:64], rim_next[208:256]], axis=0)
            owned_weight = jnp.concatenate([weight[0:64], weight[208:256]], axis=0)
            grams = tuple(a + b for a, b in zip(grams, gram(owned, owned_weight)))
        else:
            rounded[rim] = rim_next.astype(BF16)
    return grams, everything


def rotate_phase(filtered, factor, out):
    result = dot3(filtered, factor)
    for (x, y), start in STARTS.items():
        column = jnp.concatenate(
            [result[start : start + 6], result[start + 7 : start + 12]], axis=0
        )
        out[x, y] = column.astype(BF16)


def greet(peers):
    barrier = pltpu.get_barrier_semaphore()
    for peer in peers:
        pl.semaphore_signal(barrier, inc=1, device_id=peer, device_id_type=pl.DeviceIdType.MESH)
    return lambda: pl.semaphore_wait(barrier, len(peers))


def halo_offsets():
    return [(dx, dy) for dx, dy, _, _ in MESSAGES]


def at_offset(sizes, offset):
    n_gx, n_gy = sizes
    return (
        lax.rem(lax.axis_index("gx") + (offset[0] + n_gx), n_gx),
        lax.rem(lax.axis_index("gy") + (offset[1] + n_gy), n_gy),
    )


def fused_kernel(sizes, node_total, orbitals, masses, cells, to_rows, to_columns, pick_xy, pick_z,
                 out, matrix, mass_pad, states, rounded, sent, arrived, send_sems, recv_sems,
                 own, row_in, part, column_in, whole,
                 row_send, row_recv, col_send, col_recv, all_send, all_recv):
    n_gx, n_gy = sizes
    my_y = lax.axis_index("gy")
    offsets = {(dx % n_gx, dy % n_gy) for dx, dy in halo_offsets()}
    offsets |= {(0, d) for d in range(1, n_gy)} | {(d, 0) for d in range(1, n_gx)}
    wait_all = greet([at_offset(sizes, offset) for offset in sorted(offsets)])
    grams, moves = filter_phase(
        sizes, orbitals, masses, cells, to_rows, to_columns, pick_xy, pick_z,
        matrix, mass_pad, states, rounded, sent, arrived, send_sems, recv_sems, wait_all,
    )
    chunk = own.shape[1]
    per_block = 128 // chunk if 128 % chunk == 0 else None
    stacked = jnp.concatenate(grams, axis=0)
    for index in range(n_gy):
        own[index] = stacked[index * chunk : (index + 1) * chunk]

    def remote(src, dst, send, recv, offset):
        return pltpu.make_async_remote_copy(
            src_ref=src, dst_ref=dst, send_sem=send, recv_sem=recv,
            device_id=at_offset(sizes, offset), device_id_type=pl.DeviceIdType.MESH,
        )

    row_moves = [
        remote(own.at[lax.rem(my_y + d, n_gy)], row_in.at[d - 1], row_send.at[d - 1],
               row_recv.at[d - 1], (0, d))
        for d in range(1, n_gy)
    ]
    for move in row_moves:
        move.start()
    for move in row_moves:
        move.wait_recv()
    total = own[my_y]
    for d in range(1, n_gy):
        total = total + row_in[d - 1]
    part[...] = total
    col_moves = [
        remote(part, column_in.at[d - 1], col_send.at[d - 1], col_recv.at[d - 1], (d, 0))
        for d in range(1, n_gx)
    ]
    for move in col_moves:
        move.start()
    for move in col_moves:
        move.wait_recv()
    for d in range(1, n_gx):
        total = total + column_in[d - 1]
    whole[my_y] = total
    all_moves = [
        remote(whole.at[my_y], whole.at[my_y], all_send.at[d - 1], all_recv.at[d - 1], (0, d))
        for d in range(1, n_gy)
    ]
    for move in all_moves:
        move.start()
    for move in all_moves:
        move.wait_recv()
    stacked = jnp.concatenate([whole[index] for index in range(n_gy)], axis=0)
    factor = inverse_root(stacked, node_total)
    rotate_phase(states[FILTER_DEG], factor, out)
    for move in moves + row_moves + col_moves + all_moves:
        move.wait_send()


def filter_kernel(sizes, orbitals, masses, cells, to_rows, to_columns, pick_xy, pick_z,
                  filtered, stacked, matrix, mass_pad, states, rounded, sent, arrived,
                  send_sems, recv_sems):
    wait_all = greet([at_offset(sizes, offset) for offset in halo_offsets()])
    grams, moves = filter_phase(
        sizes, orbitals, masses, cells, to_rows, to_columns, pick_xy, pick_z,
        matrix, mass_pad, states, rounded, sent, arrived, send_sems, recv_sems, wait_all,
    )
    stacked[...] = jnp.concatenate(grams, axis=0)
    filtered[...] = states[FILTER_DEG]
    for move in moves:
        move.wait_send()


def rotate_kernel(node_total, filtered, stacked, out):
    rotate_phase(filtered[...], inverse_root(stacked[...], node_total), out)


def body(orbitals, masses, cell_matrices):
    n_gx, n_gy = lax.axis_size("gx"), lax.axis_size("gy")
    sizes = (n_gx, n_gy)
    assert orbitals.shape == (6, 6, 11, 256) and cell_matrices.shape == (1, 1, 2, 216, 216)
    node_total = 5 * n_gx * 5 * n_gy * 11
    constants = tuple(jnp.asarray(t) for t in tables())
    vmem = pl.BlockSpec(memory_space=pltpu.VMEM)
    count = len(MESSAGES)
    filter_scratch = [
        pltpu.VMEM((ROWS, ROWS), BF16),
        pltpu.VMEM((48, 128), F32),
        pltpu.VMEM((FILTER_DEG + 1, ROWS, 256), F32),
        pltpu.VMEM((ROWS, 256), BF16),
        pltpu.VMEM((FILTER_DEG, RIM + CORNER, 256), F32),
        pltpu.VMEM((FILTER_DEG, 384, 256), F32),
        pltpu.SemaphoreType.DMA((FILTER_DEG, count)),
        pltpu.SemaphoreType.DMA((FILTER_DEG, count)),
    ]
    params = pltpu.CompilerParams(
        collective_id=0, has_side_effects=True, vmem_limit_bytes=48 << 20
    )
    if 384 % (8 * n_gy) == 0:
        chunk = 384 // n_gy
        return pl.pallas_call(
            functools.partial(fused_kernel, sizes, node_total),
            out_shape=jax.ShapeDtypeStruct(orbitals.shape, BF16),
            in_specs=[vmem] * 7,
            out_specs=vmem,
            scratch_shapes=filter_scratch
            + [
                pltpu.VMEM((n_gy, chunk, 128), F32),
                pltpu.VMEM((n_gy - 1, chunk, 128), F32),
                pltpu.VMEM((chunk, 128), F32),
                pltpu.VMEM((n_gx - 1, chunk, 128), F32),
                pltpu.VMEM((n_gy, chunk, 128), F32),
                pltpu.SemaphoreType.DMA((n_gy - 1,)),
                pltpu.SemaphoreType.DMA((n_gy - 1,)),
                pltpu.SemaphoreType.DMA((n_gx - 1,)),
                pltpu.SemaphoreType.DMA((n_gx - 1,)),
                pltpu.SemaphoreType.DMA((n_gy - 1,)),
                pltpu.SemaphoreType.DMA((n_gy - 1,)),
            ],
            compiler_params=params,
        )(orbitals, masses, cell_matrices, *constants)
    filtered, stacked = pl.pallas_call(
        functools.partial(filter_kernel, sizes),
        out_shape=[
            jax.ShapeDtypeStruct((ROWS, 256), F32),
            jax.ShapeDtypeStruct((384, 128), F32),
        ],
        in_specs=[vmem] * 7,
        out_specs=[vmem] * 2,
        scratch_shapes=filter_scratch,
        compiler_params=params,
    )(orbitals, masses, cell_matrices, *constants)
    stacked = lax.psum(stacked, ("gx", "gy"))
    return pl.pallas_call(
        functools.partial(rotate_kernel, node_total),
        out_shape=jax.ShapeDtypeStruct(orbitals.shape, BF16),
        in_specs=[vmem] * 2,
        out_specs=vmem,
        compiler_params=pltpu.CompilerParams(vmem_limit_bytes=48 << 20),
    )(filtered, stacked)


def solution(mesh):
    return jax.shard_map(
        body,
        mesh=mesh,
        in_specs=(P("gx", "gy", None, None), P("gx", "gy", None), P("gx", "gy", None, None, None)),
        out_specs=P("gx", "gy", None, None),
        check_vma=False,
    )
```

time: 196 us -> 50.5 us (0.26)
  waiting for transfers between devices: 126 us -> 0 us
  Pallas kernels: 0 us -> 44.3 us
  starting transfers between devices: 17.1 us -> 0 us
  between operations: 15.3 us -> 0.02 us
  local copies, waits for them, and re-layouts: 21 us -> 5.86 us
  other arithmetic: 11.6 us -> 0 us
  matrix products: 4.74 us -> 0 us
    psum x2 -> x0, waiting for transfers between devices: 90.9 us -> none  [the longest x1 53.8 us: body(): row_sum = lax.psum(local_intersection, 'gy')]
    pallas_call x0 -> x1, Pallas kernels: none -> 44.3 us  [body(): pl.pallas_call(functools.partial(fused_kernel, sizes, node_total), out_sh...]
    ppermute x12 -> x0, waiting for transfers between devices: 35.1 us -> none  [the longest x6 27 us: with_halo(): before = lax.ppermute(last, axis, up)]
    ppermute x12 -> x0, starting transfers between devices: 17 us -> none  [the longest x6 13.6 us: with_halo(): after = lax.ppermute(leading, axis, down)]
    scatter-add x30 -> x0, other arithmetic: 7.44 us -> none  [the longest x6 5.81 us: apply_operator(): summed = summed.at[0, 0].add(padded[0, 0]).at[0, -1].add(padded[0, -1])]
    slice x32 -> x0, local copies, waits for them, and re-layouts: 4.87 us -> none  [the longest x9 2.14 us: fold_cells(): moved[:, 5]]
    dot_general x10 -> x0, matrix products: 4.74 us -> none  [the longest x1 1.86 us: body(): jnp.einsum('no,np->op', owned_rows * owned_mass, owned_rows, precision=la...]
    scatter-add x9 -> x0, local copies, waits for them, and re-layouts: 4.14 us -> none  [fold_cells(): leading = leading.at[:, 0].add(carried)]
  transfers between devices with their start and end apart: 14 -> 0, of which waited for: 11 -> 0; matrix products, arithmetic and copies ran while one was open for 1% -> 0% of each run, Pallas kernels for 0% -> 0%
where the time goes in v1:
time: 50.5 us; the launch traced here: 50.2 us
  Pallas kernels  44.3 us (88%)
  local copies, waits for them, and re-layouts  5.86 us (12%)
    pallas_call x1, Pallas kernels, body(): pl.pallas_call(functools.partial(fused_kernel, sizes, node_total), out_sh...  44.3 us
    unnamed x13, local copies, waits for them, and re-layouts  5.08 us

profile of v1, /device:TPU:0, one launch (start us, length us, event | category | flops | bytes accessed | tf_op | source)
XLA Modules:
  0.0 50.2 jit_solution(9388961453664365267)
XLA Ops:
  0.0 0.0 copy-start.1
  0.0 0.0 copy-start.5
  0.0 1.1 %copy.8.orbitals = bf16[6,6,11,256]{3,2,1,0:T(8,128)(2,1)S(1)} copy(bf16[6,6,11,256]{3,1,2,0:T(8,128)(2,1)} %param.7) | data formatting | bytes 405504 | tf_op args[0]
  1.1 0.0 copy-done.1
  1.1 0.0 copy-done.5
  1.1 0.0 copy-start
  1.1 1.1 %copy-done = f32[3,448,128]{2,1,0:T(8,128)S(1)} copy-done((f32[3,448,128]{2,1,0:T(8,128)S(1)}, f32[3,448,128]{2,1,0:T(8,128)}, u32[]{:S(2)}) %copy-start) | copy-done | bytes 688152
  2.2 0.0 copy-start.2
  2.2 1.0 %copy-done.2 = bf16[2,216,448]{2,1,0:T(8,128)(2,1)S(1)} copy-done((bf16[2,216,448]{2,1,0:T(8,128)(2,1)S(1)}, bf16[2,216,448]{2,1,0:T(8,128)(2,1)}, u32[]{:S(2)}) %copy-start.2) | copy-done | bytes 387096
  3.2 0.0 copy-start.3
  3.2 0.9 %copy-done.3 = f32[448,48]{1,0:T(8,128)S(1)} copy-done((f32[448,48]{1,0:T(8,128)S(1)}, f32[448,48]{1,0:T(8,128)}, u32[]{:S(2)}) %copy-start.3) | copy-done | bytes 86040
  4.2 0.0 copy-start.4
  4.2 0.9 %copy-done.4 = bf16[1,1,2,216,216]{4,3,2,1,0:T(8,128)(2,1)S(1)} copy-done((bf16[1,1,2,216,216]{4,3,2,1,0:T(8,128)(2,1)S(1)}, bf16[1,1,2,216,216]{4,3,2,1,0:T(8,128)(2,1)}, u32[]{:S(2)}) %copy-start.4) | copy-done | bytes 186648
  5.1 44.3 %shard_map.73 = bf16[6,6,11,256]{3,2,1,0:T(8,128)(2,1)S(1)} custom-call(bf16[6,6,11,256]{3,2,1,0:T(8,128)(2,1)S(1)} %copy.8.orbitals, f32[6,6,11]{2,1,0:T(8,128)S(1)} %copy-done.5, bf16[1,1,2,216,216]{4,3,2,1,0:T(8,128)(2,1)S(1)} %copy-done.4, bf16[2,448,216]{2,1,0:T(8,128)(2,1)S(1)} %copy-done.1, bf16[2,216,448]{2,1,0:T(8,128)(2,1)S(1)} %copy-done.2, ...), custom_call_target="tpu_custom_call" | custom-call | tf_op jit(solution)/shard_map/pallas_call | solution.py:368
  49.4 0.8 %copy.9 = bf16[6,6,11,256]{3,1,2,0:T(8,128)(2,1)} copy(bf16[6,6,11,256]{3,2,1,0:T(8,128)(2,1)S(1)} %shard_map.73) | data formatting | bytes 405504 | tf_op jit(solution)/shard_map/pallas_call | solution.py:368
Async XLA Ops:
  0.0 1.1 %copy-start.1 = (bf16[2,448,216]{2,1,0:T(8,128)(2,1)S(1)}, bf16[2,448,216]{2,1,0:T(8,128)(2,1)}, u32[]{:S(2)}) copy-start(bf16[2,448,216]{2,1,0:T(8,128)(2,1)} %constant.8.clone.to_rows) | copy-start | bytes 1161220
  0.0 1.1 %copy-start.5 = (f32[6,6,11]{2,1,0:T(8,128)S(1)}, f32[6,6,11]{2,1,0:T(8,128)}, u32[]{:S(2)}) copy-start(f32[6,6,11]{2,1,0:T(8,128)} %masses.1) | copy-start | bytes 4756
  1.1 1.1 %copy-start = (f32[3,448,128]{2,1,0:T(8,128)S(1)}, f32[3,448,128]{2,1,0:T(8,128)}, u32[]{:S(2)}) copy-start(f32[3,448,128]{2,1,0:T(8,128)} %constant.11.clone.pick_z) | copy-start | bytes 2064388
  2.2 1.0 %copy-start.2 = (bf16[2,216,448]{2,1,0:T(8,128)(2,1)S(1)}, bf16[2,216,448]{2,1,0:T(8,128)(2,1)}, u32[]{:S(2)}) copy-start(bf16[2,216,448]{2,1,0:T(8,128)(2,1)} %constant.9.clone.to_columns) | copy-start | bytes 1161220
  3.2 0.9 %copy-start.3 = (f32[448,48]{1,0:T(8,128)S(1)}, f32[448,48]{1,0:T(8,128)}, u32[]{:S(2)}) copy-start(f32[448,48]{1,0:T(8,128)} %constant.10.clone.pick_xy) | copy-start | bytes 258052
  4.2 0.9 %copy-start.4 = (bf16[1,1,2,216,216]{4,3,2,1,0:T(8,128)(2,1)S(1)}, bf16[1,1,2,216,216]{4,3,2,1,0:T(8,128)(2,1)}, u32[]{:S(2)}) copy-start(bf16[1,1,2,216,216]{4,3,2,1,0:T(8,128)(2,1)} %cells.1) | copy-start | bytes 559876

commit v2 on v0

v2 whole, which is shorter than its diff:
```python
import functools

import jax
import jax.numpy as jnp
import numpy as np
from jax import lax
from jax.experimental import pallas as pl
from jax.experimental.pallas import tpu as pltpu
from jax.sharding import PartitionSpec as P

FILTER_DEG = 3
CENTER_SHIFT = 12.0
HALF_SPAN = 12.0

RIM = 240
ROWS = 432
INNER = ROWS - RIM
CORNERS = 48
PIECES = 1
VMEM_BYTES = (64 << 20) - (128 << 10)
BF16 = jnp.bfloat16
F32 = jnp.float32

MESSAGES = (
    (-1, -1, "corner", 0, 3),
    (1, -1, "corner", 1, 2),
    (-1, 1, "corner", 2, 1),
    (1, 1, "corner", 3, 0),
    (-1, 0, "x", 0, 1),
    (1, 0, "x", 1, 0),
    (0, -1, "y", 0, 1),
    (0, 1, "y", 1, 0),
)


def column_starts():
    starts = {(0, 0): 0, (5, 0): 12, (0, 5): 24, (5, 5): 36}
    for i in range(4):
        starts[(0, i + 1)] = 48 + 12 * i
        starts[(5, i + 1)] = 96 + 12 * i
        starts[(i + 1, 0)] = 144 + 12 * i
        starts[(i + 1, 5)] = 192 + 12 * i
    for i in range(4):
        for j in range(4):
            starts[(i + 1, j + 1)] = RIM + 12 * (4 * i + j)
    return starts


STARTS = column_starts()


def tables():
    down = np.zeros((ROWS, 128), np.int32)
    along = np.full((8, ROWS), -1, np.int32)
    for (x, y), start in STARTS.items():
        for half in range(2):
            for k in range(6):
                row, z = start + 6 * half + k, 5 * half + k
                for cell in range(2):
                    inside = 0 <= z - 5 * cell <= 5
                    down[row, cell] = (x * 6 + y) * 6 + z - 5 * cell if inside else -1
                down[row, 2], down[row, 3] = 8 * x + y, z
                down[row, 4] = int(x < 5 and y < 5 and not (half == 1 and k == 0))
                along[half, row] = (x * 6 + y) * 6 + k
    return down, along


def dot(a, b):
    return jnp.dot(a, b, preferred_element_type=F32)


def dot_rows(a, b):
    return lax.dot_general(a, b, (((0,), (0,)), ((), ())), preferred_element_type=F32)


def split(a):
    high = a.astype(BF16)
    return high, (a - high.astype(F32)).astype(BF16)


def dot3(a, b):
    a_high, a_low = split(a)
    b_high, b_low = split(b)
    return dot(a_high, b_high) + (dot(a_high, b_low) + dot(a_low, b_high))


def one_hot(condition):
    return jnp.where(condition, 1.0, 0.0).astype(F32)


def gram(rows, weight):
    a_high, a_low = split(rows * weight)
    b_high, b_low = split(rows)

    def part(lanes, columns):
        return dot_rows(a_high[:, lanes], b_high[:, columns]) + (
            dot_rows(a_high[:, lanes], b_low[:, columns])
            + dot_rows(a_low[:, lanes], b_high[:, columns])
        )

    top = part(slice(0, 128), slice(0, 256))
    return top[:, :128], top[:, 128:], part(slice(128, 256), slice(128, 256))


def inverse_root(stacked, node_total):
    s00, s01, s11 = stacked[0:128], stacked[128:256], stacked[256:384]
    top = jnp.concatenate([s00, s01], axis=1)
    bottom = jnp.concatenate([s01.T, s11], axis=1)
    inter = jnp.concatenate([top, bottom], axis=0) * (1.0 / node_total)
    frob2 = jnp.sum(jnp.sum(inter * inter, axis=1, keepdims=True), axis=0, keepdims=True)
    frob = jnp.sqrt(frob2)
    current = inter / frob
    row_id = lax.broadcasted_iota(jnp.int32, (256, 256), 0)
    col_id = lax.broadcasted_iota(jnp.int32, (256, 256), 1)
    identity = one_hot(row_id == col_id)
    square = dot3(current, current)
    tail = 1.6875 * identity - 0.5625 * current + 0.0625 * square
    factor_z = 2.25 * identity - 2.4375 * current + dot3(square, tail)
    return factor_z / jnp.sqrt(frob)


def at_offset(sizes, offset):
    n_gx, n_gy = sizes
    return (
        lax.rem(lax.axis_index("gx") + (offset[0] + n_gx), n_gx),
        lax.rem(lax.axis_index("gy") + (offset[1] + n_gy), n_gy),
    )


def remote(sizes, src, dst, send, recv, offset):
    return pltpu.make_async_remote_copy(
        src_ref=src, dst_ref=dst, send_sem=send, recv_sem=recv,
        device_id=at_offset(sizes, offset), device_id_type=pl.DeviceIdType.MESH,
    )


def greet(sizes, offsets):
    barrier = pltpu.get_barrier_semaphore()
    offsets = sorted({(dx % sizes[0], dy % sizes[1]) for dx, dy in offsets})
    for offset in offsets:
        pl.semaphore_signal(
            barrier, inc=1, device_id=at_offset(sizes, offset),
            device_id_type=pl.DeviceIdType.MESH,
        )
    return lambda: pl.semaphore_wait(barrier, len(offsets))


HALO_OFFSETS = [(dx, dy) for dx, dy, _, _, _ in MESSAGES]


def filter_phase(sizes, inputs, scratch, ready):
    (nodes_in, masses_in, cells_in, down_in, along_in) = inputs
    (nodes, masses, cells, down, along, padded, mass_pad, rim_matrix, inner_matrix, states,
     rim_rounded, inner_rounded, sums, sent_x, sent_y, sent_corner, got_x, got_y, got_corner,
     load_sems, send_sems, recv_sems) = scratch

    loads = [
        pltpu.make_async_copy(src, dst, load_sems.at[index])
        for index, (src, dst) in enumerate(
            [(down_in, down), (along_in, along), (cells_in, cells), (masses_in, masses),
             (nodes_in, nodes)]
        )
    ]
    for load in loads:
        load.start()
    loads[0].wait()
    loads[1].wait()

    lanes = lax.broadcasted_iota(jnp.int32, (ROWS, 216), 1)
    to_rows = [one_hot(lanes == down[:, c : c + 1]).astype(BF16) for c in range(2)]
    places = lax.broadcasted_iota(jnp.int32, (216, ROWS), 0)
    to_columns = [one_hot(places == along[c : c + 1, :]).astype(BF16) for c in range(2)]

    loads[2].wait()
    first = dot(to_rows[0], cells[0, 0, 0]).astype(BF16)
    second = dot(to_rows[1], cells[0, 0, 1]).astype(BF16)
    matrix = (dot(first, to_columns[0]) + dot(second, to_columns[1])).astype(BF16)
    rim_matrix[...] = matrix[:, :RIM]
    inner_matrix[...] = matrix[:, RIM:]

    loads[3].wait()
    mass_pad[...] = jnp.zeros(mass_pad.shape, F32)
    for x in range(6):
        high, rest = split(masses[x])
        low, least = split(masses[x] - high.astype(F32))
        mass_pad[8 * x : 8 * x + 6, 0:11] = high.astype(F32)
        mass_pad[8 * x : 8 * x + 6, 16:27] = low.astype(F32)
        mass_pad[8 * x : 8 * x + 6, 32:43] = least.astype(F32)
    pick = one_hot(lax.broadcasted_iota(jnp.int32, (ROWS, 48), 1) == down[:, 2:3]).astype(BF16)
    spread = dot(pick, mass_pad[...].astype(BF16))
    lane = lax.broadcasted_iota(jnp.int32, (ROWS, 128), 1)
    mass = jnp.sum(
        jnp.where(lane % 16 == down[:, 3:4], spread, 0.0), axis=1, keepdims=True
    )
    weight = mass * down[:, 4:5].astype(F32)
    scale1 = 1.0 / (HALF_SPAN * mass)
    shift = CENTER_SHIFT / HALF_SPAN

    loads[4].wait()
    for x in range(6):
        for z in range(11):
            for half in range(2):
                padded[half, 8 * (11 * x + z) : 8 * (11 * x + z) + 6] = nodes[
                    x, z, :, 128 * half : 128 * half + 128
                ].astype(F32)
    for (x, y), start in STARTS.items():
        for half in range(2):
            for low, skip in ((0, 0), (6, 40)):
                states[0, half, start + low : start + low + 6] = padded[
                    half, pl.ds(88 * x + skip + y, 6, stride=8)
                ]
    rim, inner = slice(0, RIM), slice(RIM, ROWS)
    for half in range(2):
        rim_rounded[half] = states[0, half, rim].astype(BF16)
        inner_rounded[half] = states[0, half, inner].astype(BF16)

    buffers = {"x": (sent_x, got_x), "y": (sent_y, got_y), "corner": (sent_corner, got_corner)}

    def moves_of(step, half):
        return [
            remote(
                sizes, buffers[kind][0].at[step, half, here], buffers[kind][1].at[step, half, there],
                send_sems.at[step, half, index], recv_sems.at[step, half, index], (dx, dy),
            )
            for index, (dx, dy, kind, here, there) in enumerate(MESSAGES)
        ]

    def advance(step, half, product, rows):
        if step == 0:
            return product * scale1[rows] - shift * states[0, half, rows]
        return (
            (2.0 * product) * scale1[rows]
            - (2.0 * shift) * states[step, half, rows]
            - states[step - 1, half, rows]
        )

    moves = {}

    def launch(step, half, ahead):
        product = ahead + dot(rim_matrix[rim], rim_rounded[half])
        sums[step, half] = product
        corners = [product[12 * i : 12 * i + 12] for i in range(4)]
        for i in range(4):
            sent_corner[step, half, i] = corners[i]
        sent_x[step, half, 0] = jnp.concatenate([corners[0], corners[2], product[48:96]], axis=0)
        sent_x[step, half, 1] = jnp.concatenate([corners[1], corners[3], product[96:144]], axis=0)
        sent_y[step, half, 0] = jnp.concatenate([product[0:24], product[144:192]], axis=0)
        sent_y[step, half, 1] = jnp.concatenate([product[24:48], product[192:240]], axis=0)
        if step == 0 and half == 0:
            ready()
        moves[step, half] = moves_of(step, half)
        for move in moves[step, half]:
            move.start()

    def inside(step, half):
        inner_next = advance(
            step,
            half,
            dot(rim_matrix[inner], rim_rounded[half])
            + dot(inner_matrix[inner], inner_rounded[half]),
            inner,
        )
        states[step + 1, half, inner] = inner_next
        if step == FILTER_DEG - 1:
            return inner_next
        inner_rounded[half] = inner_next.astype(BF16)
        return dot(inner_matrix[rim], inner_rounded[half])

    def finish(step, half):
        for move in moves[step, half]:
            move.wait_recv()
        own = sums[step, half]
        x0, x5 = got_x[step, half, 0], got_x[step, half, 1]
        y0, y5 = got_y[step, half, 0], got_y[step, half, 1]
        far = [got_corner[step, half, i] for i in range(4)]
        theirs = jnp.concatenate(
            [
                x0[0:12] + y0[0:12] + far[0],
                x5[0:12] + y0[12:24] + far[1],
                x0[12:24] + y5[0:12] + far[2],
                x5[12:24] + y5[12:24] + far[3],
                x0[24:72],
                x5[24:72],
                y0[24:72],
                y5[24:72],
            ],
            axis=0,
        )
        rim_next = advance(step, half, own + theirs, rim)
        states[step + 1, half, rim] = rim_next
        rim_rounded[half] = rim_next.astype(BF16)
        return rim_next

    for half in range(2):
        launch(0, half, dot(inner_matrix[rim], inner_rounded[half]))
    ahead = [inside(0, half) for half in range(2)]
    for step in range(FILTER_DEG - 1):
        for half in range(2):
            finish(step, half)
            launch(step + 1, half, ahead[half])
            ahead[half] = inside(step + 1, half)
    grams = gram(jnp.concatenate(ahead, axis=1), weight[inner])
    keep = lambda a: jnp.concatenate([a[0:24], a[48:96], a[144:192]], axis=0)
    rims = [keep(finish(FILTER_DEG - 1, half)) for half in range(2)]
    rim_grams = gram(jnp.concatenate(rims, axis=1), keep(weight[rim]))
    return tuple(a + b for a, b in zip(grams, rim_grams)), sum(moves.values(), [])


def whole_rows(states):
    return jnp.concatenate([states[FILTER_DEG, 0], states[FILTER_DEG, 1]], axis=1)


def rotate_phase(filtered, factor, padded, out):
    result = dot3(filtered, factor)
    for (x, y), start in STARTS.items():
        for half in range(2):
            lanes = slice(128 * half, 128 * half + 128)
            padded[half, pl.ds(88 * x + y, 6, stride=8)] = result[start : start + 6, lanes]
            padded[half, pl.ds(88 * x + 48 + y, 5, stride=8)] = result[
                start + 7 : start + 12, lanes
            ]
    for x in range(6):
        for z in range(11):
            low = 8 * (11 * x + z)
            out[x, z] = jnp.concatenate(
                [padded[0, low : low + 6], padded[1, low : low + 6]], axis=1
            ).astype(BF16)


def fused_kernel(sizes, node_total, *refs):
    inputs, out, scratch, extra = refs[:5], refs[5], refs[6:28], refs[28:]
    (own, row_in, part, column_in, whole,
     row_send, row_recv, col_send, col_recv, all_send, all_recv) = extra
    n_gx, n_gy = sizes
    my_y = lax.axis_index("gy")
    ready = greet(
        sizes,
        HALO_OFFSETS + [(0, d) for d in range(1, n_gy)] + [(d, 0) for d in range(1, n_gx)],
    )
    grams, moves = filter_phase(sizes, inputs, scratch, ready)
    pieces, height = own.shape[0], own.shape[2]
    stacked = jnp.concatenate(grams, axis=0)
    row_moves, col_moves, all_moves = [], [], []
    for p in range(pieces):
        for index in range(n_gy):
            low = (index * pieces + p) * height
            own[p, index] = stacked[low : low + height]
        row_moves.append([
            remote(sizes, own.at[p, lax.rem(my_y + d, n_gy)], row_in.at[p, d - 1],
                   row_send.at[p, d - 1], row_recv.at[p, d - 1], (0, d))
            for d in range(1, n_gy)
        ])
        for move in row_moves[p]:
            move.start()
        col_moves.append([
            remote(sizes, part.at[p], column_in.at[p, d - 1],
                   col_send.at[p, d - 1], col_recv.at[p, d - 1], (d, 0))
            for d in range(1, n_gx)
        ])
        all_moves.append([
            remote(sizes, whole.at[p, my_y], whole.at[p, my_y],
                   all_send.at[p, d - 1], all_recv.at[p, d - 1], (0, d))
            for d in range(1, n_gy)
        ])

    def second(p):
        for move in row_moves[p]:
            move.wait_recv()
        total = own[p, my_y]
        for d in range(1, n_gy):
            total = total + row_in[p, d - 1]
        part[p] = total
        for move in col_moves[p]:
            move.start()

    def third(p):
        for move in col_moves[p]:
            move.wait_recv()
        total = part[p]
        for d in range(1, n_gx):
            total = total + column_in[p, d - 1]
        whole[p, my_y] = total
        for move in all_moves[p]:
            move.start()

    for p in range(pieces):
        second(p)
        if p >= 1:
            third(p - 1)
    third(pieces - 1)
    for p in range(pieces):
        for move in all_moves[p]:
            move.wait_recv()
    stacked = jnp.concatenate(
        [whole[p, index] for index in range(n_gy) for p in range(pieces)], axis=0
    )
    factor = inverse_root(stacked, node_total)
    rotate_phase(whole_rows(scratch[9]), factor, scratch[5], out)
    for move in moves + sum(row_moves + col_moves + all_moves, []):
        move.wait_send()


def filter_kernel(sizes, *refs):
    inputs, filtered, stacked, scratch = refs[:5], refs[5], refs[6], refs[7:]
    grams, moves = filter_phase(sizes, inputs, scratch, greet(sizes, HALO_OFFSETS))
    stacked[...] = jnp.concatenate(grams, axis=0)
    filtered[...] = whole_rows(scratch[9])
    for move in moves:
        move.wait_send()


def rotate_kernel(node_total, filtered, stacked, out, padded):
    rotate_phase(filtered[...], inverse_root(stacked[...], node_total), padded, out)


def body(orbitals, masses, cell_matrices):
    n_gx, n_gy = lax.axis_size("gx"), lax.axis_size("gy")
    sizes = (n_gx, n_gy)
    assert orbitals.shape == (6, 6, 11, 256) and cell_matrices.shape == (1, 1, 2, 216, 216)
    node_total = 5 * n_gx * 5 * n_gy * 11
    nodes = jnp.transpose(orbitals, (0, 2, 1, 3))
    down, along = tables()
    arguments = (nodes, masses, cell_matrices, jnp.asarray(down), jnp.asarray(along))
    vmem = pl.BlockSpec(memory_space=pltpu.VMEM)
    hbm = pl.BlockSpec(memory_space=pltpu.MemorySpace.HBM)
    filter_scratch = [
        pltpu.VMEM(nodes.shape, BF16),
        pltpu.VMEM(masses.shape, F32),
        pltpu.VMEM(cell_matrices.shape, BF16),
        pltpu.VMEM(down.shape, jnp.int32),
        pltpu.VMEM(along.shape, jnp.int32),
        pltpu.VMEM((2, 528, 128), F32),
        pltpu.VMEM((48, 128), F32),
        pltpu.VMEM((ROWS, RIM), BF16),
        pltpu.VMEM((ROWS, INNER), BF16),
        pltpu.VMEM((FILTER_DEG + 1, 2, ROWS, 128), F32),
        pltpu.VMEM((2, RIM, 128), BF16),
        pltpu.VMEM((2, INNER, 128), BF16),
        pltpu.VMEM((FILTER_DEG, 2, RIM, 128), F32),
    ]
    filter_scratch += [
        pltpu.VMEM((FILTER_DEG, 2) + shape + (128,), F32)
        for shape in ((2, 72), (2, 72), (4, 12)) * 2
    ]
    filter_scratch += [
        pltpu.SemaphoreType.DMA((5,)),
        pltpu.SemaphoreType.DMA((FILTER_DEG, 2, len(MESSAGES))),
        pltpu.SemaphoreType.DMA((FILTER_DEG, 2, len(MESSAGES))),
    ]
    params = pltpu.CompilerParams(
        collective_id=0, has_side_effects=True, vmem_limit_bytes=VMEM_BYTES
    )
    if 384 % (8 * PIECES * n_gy) == 0:
        height = 384 // n_gy // PIECES
        result = pl.pallas_call(
            functools.partial(fused_kernel, sizes, node_total),
            out_shape=jax.ShapeDtypeStruct(nodes.shape, BF16),
            in_specs=[hbm] * 5,
            out_specs=vmem,
            scratch_shapes=filter_scratch
            + [
                pltpu.VMEM((PIECES, n_gy, height, 128), F32),
                pltpu.VMEM((PIECES, n_gy - 1, height, 128), F32),
                pltpu.VMEM((PIECES, height, 128), F32),
                pltpu.VMEM((PIECES, n_gx - 1, height, 128), F32),
                pltpu.VMEM((PIECES, n_gy, height, 128), F32),
            ]
            + [pltpu.SemaphoreType.DMA((PIECES, n - 1)) for n in (n_gy, n_gy, n_gx, n_gx, n_gy, n_gy)],
            compiler_params=params,
        )(*arguments)
    else:
        filtered, stacked = pl.pallas_call(
            functools.partial(filter_kernel, sizes),
            out_shape=[
                jax.ShapeDtypeStruct((ROWS, 256), F32),
                jax.ShapeDtypeStruct((384, 128), F32),
            ],
            in_specs=[hbm] * 5,
            out_specs=[vmem] * 2,
            scratch_shapes=filter_scratch,
            compiler_params=params,
        )(*arguments)
        stacked = lax.psum(stacked, ("gx", "gy"))
        result = pl.pallas_call(
            functools.partial(rotate_kernel, node_total),
            out_shape=jax.ShapeDtypeStruct(nodes.shape, BF16),
            in_specs=[vmem] * 2,
            out_specs=vmem,
            scratch_shapes=[pltpu.VMEM((2, 528, 128), F32)],
            compiler_params=pltpu.CompilerParams(vmem_limit_bytes=VMEM_BYTES),
        )(filtered, stacked)
    return jnp.transpose(result, (0, 2, 1, 3))


def solution(mesh):
    return jax.shard_map(
        body,
        mesh=mesh,
        in_specs=(P("gx", "gy", None, None), P("gx", "gy", None), P("gx", "gy", None, None, None)),
        out_specs=P("gx", "gy", None, None),
        check_vma=False,
    )
```

time: 196 us -> 40.1 us (0.20)
  waiting for transfers between devices: 126 us -> 0 us
  Pallas kernels: 0 us -> 38.2 us
  local copies, waits for them, and re-layouts: 21 us -> 1.68 us
  starting transfers between devices: 17.1 us -> 0 us
  between operations: 15.3 us -> 0.01 us
  other arithmetic: 11.6 us -> 0 us
  matrix products: 4.74 us -> 0 us
    psum x2 -> x0, waiting for transfers between devices: 90.9 us -> none  [the longest x1 53.8 us: body(): row_sum = lax.psum(local_intersection, 'gy')]
    pallas_call x0 -> x1, Pallas kernels: none -> 38.2 us  [body(): pl.pallas_call(functools.partial(fused_kernel, sizes, node_total), out_sh...]
    ppermute x12 -> x0, waiting for transfers between devices: 35.1 us -> none  [the longest x6 27 us: with_halo(): before = lax.ppermute(last, axis, up)]
    ppermute x12 -> x0, starting transfers between devices: 17 us -> none  [the longest x6 13.6 us: with_halo(): after = lax.ppermute(leading, axis, down)]
    scatter-add x30 -> x0, other arithmetic: 7.44 us -> none  [the longest x6 5.81 us: apply_operator(): summed = summed.at[0, 0].add(padded[0, 0]).at[0, -1].add(padded[0, -1])]
    slice x32 -> x0, local copies, waits for them, and re-layouts: 4.87 us -> none  [the longest x9 2.14 us: fold_cells(): moved[:, 5]]
    dot_general x10 -> x0, matrix products: 4.74 us -> none  [the longest x1 1.86 us: body(): jnp.einsum('no,np->op', owned_rows * owned_mass, owned_rows, precision=la...]
    scatter-add x9 -> x0, local copies, waits for them, and re-layouts: 4.14 us -> none  [fold_cells(): leading = leading.at[:, 0].add(carried)]
  transfers between devices with their start and end apart: 14 -> 0, of which waited for: 11 -> 0; matrix products, arithmetic and copies ran while one was open for 1% -> 0% of each run, Pallas kernels for 0% -> 0%
where the time goes in v2:
time: 40.1 us; the launch traced here: 39.9 us
  Pallas kernels  38.2 us (95%)
  local copies, waits for them, and re-layouts  1.68 us (4%)
    pallas_call x1, Pallas kernels, body(): pl.pallas_call(functools.partial(fused_kernel, sizes, node_total), out_sh...  38.2 us
    unnamed x1, local copies, waits for them, and re-layouts  1.68 us

profile of v2, /device:TPU:0, one launch (start us, length us, event | category | flops | bytes accessed | tf_op | source)
XLA Modules:
  0.0 39.9 jit_solution(12158878553578602947)
XLA Ops:
  0.0 38.2 %shard_map.55 = bf16[6,11,6,256]{3,2,1,0:T(8,128)(2,1)} custom-call(bf16[6,11,6,256]{3,2,1,0:T(8,128)(2,1)} %bitcast.3, f32[6,6,11]{2,1,0:T(8,128)} %refs_1_.1, bf16[1,1,2,216,216]{4,3,2,1,0:T(8,128)(2,1)} %refs_2_.1, s32[432,128]{1,0:T(8,128)} %constant.4.clone.refs_3_, s32[8,432]{1,0:T(8,128)} %constant.5.clone.refs_4_), custom_call_target="tpu_custom_call" | custom-call | tf_op jit(solution)/shard_map/pallas_call | solution.py:455
  38.2 1.7 %copy.7 = bf16[6,6,11,256]{3,1,2,0:T(8,128)(2,1)} copy(bf16[6,6,11,256]{3,1,2,0:T(8,128)(2,1)} %bitcast.2) | data formatting | bytes 405504

commit v3 on v2

--- a/solution.py
+++ b/solution.py
@@ -100,6 +100,30 @@
 
     top = part(slice(0, 128), slice(0, 256))
     return top[:, :128], top[:, 128:], part(slice(128, 256), slice(128, 256))
+
+
+def block_ids():
+    return (
+        lax.broadcasted_iota(jnp.int32, (128, 128), 0),
+        lax.broadcasted_iota(jnp.int32, (128, 128), 1),
+    )
+
+
+def pack(grams):
+    s00, s01, s11 = grams
+    row, col = block_ids()
+    diagonal = jnp.sum(jnp.where(row == col, s11, 0.0), axis=0, keepdims=True)
+    return jnp.concatenate([s01, jnp.where(row <= col, s00, s11)], axis=0), diagonal
+
+
+def unpack(packed, diagonal):
+    s01, both = packed[0:128], packed[128:256]
+    row, col = block_ids()
+    upper = jnp.where(row <= col, both, 0.0)
+    lower = jnp.where(row > col, both, 0.0)
+    s00 = upper + jnp.where(row < col, both, 0.0).T
+    s11 = lower + lower.T + jnp.where(row == col, diagonal, 0.0)
+    return jnp.concatenate([s00, s01, s11], axis=0)
 
 
 def inverse_root(stacked, node_total):
@@ -338,13 +362,14 @@
         HALO_OFFSETS + [(0, d) for d in range(1, n_gy)] + [(d, 0) for d in range(1, n_gx)],
     )
     grams, moves = filter_phase(sizes, inputs, scratch, ready)
-    pieces, height = own.shape[0], own.shape[2]
-    stacked = jnp.concatenate(grams, axis=0)
+    pieces, height = own.shape[0], own.shape[2] - 1
+    packed, diagonal = pack(grams)
     row_moves, col_moves, all_moves = [], [], []
     for p in range(pieces):
         for index in range(n_gy):
             low = (index * pieces + p) * height
-            own[p, index] = stacked[low : low + height]
+            own[p, index, 0:height] = packed[low : low + height]
+            own[p, index, height : height + 1] = diagonal
         row_moves.append([
             remote(sizes, own.at[p, lax.rem(my_y + d, n_gy)], row_in.at[p, d - 1],
                    row_send.at[p, d - 1], row_recv.at[p, d - 1], (0, d))
@@ -391,9 +416,10 @@
     for p in range(pieces):
         for move in all_moves[p]:
             move.wait_recv()
-    stacked = jnp.concatenate(
-        [whole[p, index] for index in range(n_gy) for p in range(pieces)], axis=0
-    )
+    packed = jnp.concatenate(
+        [whole[p, index, 0:height] for index in range(n_gy) for p in range(pieces)], axis=0
+    )
+    stacked = unpack(packed, whole[0, 0, height : height + 1])
     factor = inverse_root(stacked, node_total)
     rotate_phase(whole_rows(scratch[9]), factor, scratch[5], out)
     for move in moves + sum(row_moves + col_moves + all_moves, []):
@@ -450,8 +476,8 @@
     params = pltpu.CompilerParams(
         collective_id=0, has_side_effects=True, vmem_limit_bytes=VMEM_BYTES
     )
-    if 384 % (8 * PIECES * n_gy) == 0:
-        height = 384 // n_gy // PIECES
+    if 256 % (8 * PIECES * n_gy) == 0:
+        height = 256 // n_gy // PIECES + 1
         result = pl.pallas_call(
             functools.partial(fused_kernel, sizes, node_total),
             out_shape=jax.ShapeDtypeStruct(nodes.shape, BF16),

time: 40.1 us -> 39 us (0.973)
  Pallas kernels: 38.2 us -> 37.2 us
    pallas_call x1, Pallas kernels: 38.2 us -> 37.2 us  [body(): pl.pallas_call(functools.partial(fused_kernel, sizes, node_total), out_sh...]
where the time goes in v3:
time: 39 us; the launch traced here: 38.9 us
  Pallas kernels  37.2 us (95%)
  local copies, waits for them, and re-layouts  1.68 us (4%)
    pallas_call x1, Pallas kernels, body(): pl.pallas_call(functools.partial(fused_kernel, sizes, node_total), out_sh...  37.2 us
    unnamed x1, local copies, waits for them, and re-layouts  1.68 us

profile of v3, /device:TPU:0, one launch (start us, length us, event | category | flops | bytes accessed | tf_op | source)
XLA Modules:
  0.0 38.9 jit_solution(11747223348816795389)
XLA Ops:
  0.0 37.2 %shard_map.55 = bf16[6,11,6,256]{3,2,1,0:T(8,128)(2,1)} custom-call(bf16[6,11,6,256]{3,2,1,0:T(8,128)(2,1)} %bitcast.3, f32[6,6,11]{2,1,0:T(8,128)} %refs_1_.1, bf16[1,1,2,216,216]{4,3,2,1,0:T(8,128)(2,1)} %refs_2_.1, s32[432,128]{1,0:T(8,128)} %constant.4.clone.refs_3_, s32[8,432]{1,0:T(8,128)} %constant.5.clone.refs_4_), custom_call_target="tpu_custom_call" | custom-call | tf_op jit(solution)/shard_map/pallas_call | solution.py:481
  37.2 1.7 %copy.7 = bf16[6,6,11,256]{3,1,2,0:T(8,128)(2,1)} copy(bf16[6,6,11,256]{3,1,2,0:T(8,128)(2,1)} %bitcast.2) | data formatting | bytes 405504

commit v4 on v3

--- a/solution.py
+++ b/solution.py
@@ -322,6 +322,7 @@
         for half in range(2):
             finish(step, half)
             launch(step + 1, half, ahead[half])
+        for half in range(2):
             ahead[half] = inside(step + 1, half)
     grams = gram(jnp.concatenate(ahead, axis=1), weight[inner])
     keep = lambda a: jnp.concatenate([a[0:24], a[48:96], a[144:192]], axis=0)

time: 39 us -> 39 us (level)
  no operation moved by 1% of the time
where the time goes in v4:
time: 39 us; the launch traced here: 38.9 us
  Pallas kernels  37.2 us (95%)
  local copies, waits for them, and re-layouts  1.68 us (4%)
    pallas_call x1, Pallas kernels, body(): pl.pallas_call(functools.partial(fused_kernel, sizes, node_total), out_sh...  37.2 us
    unnamed x1, local copies, waits for them, and re-layouts  1.68 us

profile of v4, /device:TPU:0, one launch (start us, length us, event | category | flops | bytes accessed | tf_op | source)
XLA Modules:
  0.0 38.9 jit_solution(14988561333253534365)
XLA Ops:
  0.0 37.2 %shard_map.55 = bf16[6,11,6,256]{3,2,1,0:T(8,128)(2,1)} custom-call(bf16[6,11,6,256]{3,2,1,0:T(8,128)(2,1)} %bitcast.3, f32[6,6,11]{2,1,0:T(8,128)} %refs_1_.1, bf16[1,1,2,216,216]{4,3,2,1,0:T(8,128)(2,1)} %refs_2_.1, s32[432,128]{1,0:T(8,128)} %constant.4.clone.refs_3_, s32[8,432]{1,0:T(8,128)} %constant.5.clone.refs_4_), custom_call_target="tpu_custom_call" | custom-call | tf_op jit(solution)/shard_map/pallas_call | solution.py:482
  37.2 1.7 %copy.7 = bf16[6,6,11,256]{3,1,2,0:T(8,128)(2,1)} copy(bf16[6,6,11,256]{3,1,2,0:T(8,128)(2,1)} %bitcast.2) | data formatting | bytes 405504
